TPU v7x, 256 devices: a whole 4x4x8 slice. The times are simulated.
256 devices in a mesh: depth: 32 (over x, z_lo, y), cols: 8 (over z_hi, core).
Axes of the slice: x: 4, y: 4, z: 8 (z_hi: 4, z_lo: 2; z = z_hi * 2 + z_lo), core: 2. Of those that a mesh axis runs over, the one named last changes fastest.
Arguments:
- amplitudes: float32 [2304, 32768], P('cols', 'depth'), may hold values from -6 to 6
- integrals: float32 [32768, 8192], P('depth', 'cols'), may hold values from -0.03125 to 0.03125
- residual_in: float32 [2304, 8192], P('depth', 'cols'), may hold values from -4 to 4
Outputs:
- residual_out: float32 [2304, 8192], P('depth', 'cols')
All inputs are finite; a program needn't handle non-finite values.
Results may differ from a plain program's by a relative error of at most 0.000071.
Values sent between devices are 32-bit elements; how exact they have to be, the bound alone decides.
A program may use at most 64 MiB of HBM per device.

v0:
```python
import jax
import jax.numpy as jnp
from jax import lax
from jax.sharding import PartitionSpec as P


def shards(amplitudes, integrals, residual_in):
    panel = lax.all_gather(amplitudes, "cols", axis=0, tiled=True)
    partial_value = jnp.dot(
        panel, integrals, precision=lax.Precision.HIGHEST, preferred_element_type=jnp.float32
    )
    owned = lax.psum_scatter(partial_value, "depth", scatter_dimension=0, tiled=True)
    return residual_in + owned


def solution(mesh):
    placed = (P("cols", "depth"), P("depth", "cols"), P("depth", "cols"))
    return jax.shard_map(
        shards, mesh=mesh, in_specs=placed, out_specs=P("depth", "cols"), check_vma=False
    )
```

profile of v0, /device:TPU:64, one launch (start us, length us, event | category | flops | bytes accessed | tf_op | source)
XLA Modules:
  0.0 334.9 jit_solution(11174748517182940044)
XLA Ops:
  6.5 0.0 all-gather.2.cloned.1.call-start
  6.5 0.7 all-gather.2.cloned.1.call-update
  7.3 0.0 reduce-scatter.2.cloned.1.call-start
  7.3 100.3 %all-gather.2.cloned.1.call-done = f32[2304,1024]{1,0:T(8,128)} async-done(((f32[288,1024]{1,0:T(8,128)}), f32[2304,1024]{1,0:T(8,128)}) %all-gather.2.cloned.1.call-update) | async-done | bytes 9437200 | tf_op jit(solution)/shard_map/all_gather | solution.py:8
  107.6 35.3 %fusion = f32[2304,1024]{1,0:T(8,128)} fusion(f32[2304,1024]{1,0:T(8,128)} %all-gather.2.cloned.1.call-done, f32[1024,1024]{1,0:T(8,128)} %param.4), kind=kOutput, calls=%fused_computation | convolution fusion | flops 28991029248 | bytes 23068672 | tf_op jit(solution)/shard_map/dot_general | solution.py:9
  142.9 0.0 copy-start
  142.9 0.0 reduce-scatter.2.cloned.1.call-update
  142.9 183.5 %reduce-scatter.2.cloned.1.call-done = f32[72,1024]{1,0:T(8,128)} async-done(((f32[2304,1024]{1,0:T(8,128)}), f32[72,1024]{1,0:T(8,128)}) %reduce-scatter.2.cloned.1.call-update) | async-done | bytes 294928 | tf_op jit(solution)/shard_map/reduce_scatter | solution.py:12
  326.4 0.0 copy-done
  326.4 1.7 add.5
Async XLA Ops:
  6.5 101.1 %all-gather.2.cloned.1.call-start = ((), (), s32[]{:S(2)}) async-start(), calls=%async_computation.1 | async-start | bytes 10616832 | tf_op jit(solution)/shard_map/all_gather | solution.py:8
  7.3 319.1 %reduce-scatter.2.cloned.1.call-start = ((), (), s32[]{:S(2)}) async-start(), calls=%async_computation.2 | async-start | bytes 9732096 | tf_op jit(solution)/shard_map/reduce_scatter | solution.py:12
  142.9 183.5 %copy-start = (f32[72,1024]{1,0:T(8,128)S(1)}, f32[72,1024]{1,0:T(8,128)}, u32[]{:S(2)}) copy-start(f32[72,1024]{1,0:T(8,128)} %param.5) | copy-start | bytes 884740
Sparse Core Ops, SparseCore 0:
  9.2 98.3 all-gather.1
  143.0 183.2 reduce-scatter.1
where the time goes:
time: 335 us
  waiting for transfers between devices  284 us (85%)
  matrix products  35.3 us (11%)
  between operations  13.4 us (4%)
    reduce_scatter x1, waiting for transfers between devices, shards(): lax.psum_scatter(partial_value, 'depth', scatter_dimension=0, tiled=True)  183 us
    all_gather x1, waiting for transfers between devices, shards(): panel = lax.all_gather(amplitudes, 'cols', axis=0, tiled=True)  100 us
    dot_general x1, matrix products, shards(): jnp.dot(panel, integrals, precision=lax.Precision.HIGHEST, preferred_elem...  35.3 us
  transfers between devices with their start and end apart: 2, of which 2 were waited for; matrix products, arithmetic and copies ran while one was open for 0% of the time, Pallas kernels for 0%

commit v1 on v0

--- a/solution.py
+++ b/solution.py
@@ -5,7 +5,9 @@
 
 
 def shards(amplitudes, integrals, residual_in):
-    panel = lax.all_gather(amplitudes, "cols", axis=0, tiled=True)
+    panel = jnp.concatenate(
+        lax.all_to_all(jnp.stack([amplitudes] * lax.axis_size("cols")), "cols", 0, 0), axis=0
+    )
     partial_value = jnp.dot(
         panel, integrals, precision=lax.Precision.HIGHEST, preferred_element_type=jnp.float32
     )

time: 335 us -> 451 us (1.35)
  blocking collectives: 0 us -> 214 us
  waiting for transfers between devices: 284 us -> 186 us
    all_to_all x0 -> x1, blocking collectives: none -> 214 us  [shards(): lax.all_to_all(jnp.stack([amplitudes] * lax.axis_size('cols')), 'cols', 0...]
    all_gather x1 -> x0, waiting for transfers between devices: 100 us -> none  [shards(): panel = lax.all_gather(amplitudes, 'cols', axis=0, tiled=True)]
  transfers between devices with their start and end apart: 2 -> 1, of which waited for: 2 -> 1; matrix products, arithmetic and copies ran while one was open for 0% -> 0% of each run, Pallas kernels for 0% -> 0%
where the time goes in v1:
time: 451 us
  blocking collectives  214 us (47%)
  waiting for transfers between devices  186 us (41%)
  matrix products  32.5 us (7%)
  between operations  13.4 us (3%)
    all_to_all x1, blocking collectives, shards(): lax.all_to_all(jnp.stack([amplitudes] * lax.axis_size('cols')), 'cols', 0...  214 us
    reduce_scatter x1, waiting for transfers between devices, shards(): lax.psum_scatter(partial_value, 'depth', scatter_dimension=0, tiled=True)  186 us
    dot_general x1, matrix products, shards(): jnp.dot(panel, integrals, precision=lax.Precision.HIGHEST, preferred_elem...  32.5 us
  transfers between devices with their start and end apart: 1, of which 1 were waited for; matrix products, arithmetic and copies ran while one was open for 0% of the time, Pallas kernels for 0%

profile of v1, /device:TPU:64, one launch (start us, length us, event | category | flops | bytes accessed | tf_op | source)
XLA Modules:
  0.0 450.7 jit_solution(5448672744346460753)
XLA Ops:
  6.5 0.0 reduce-scatter.2.cloned.1.call-start
  6.5 2.5 stack.2
  9.0 0.0 copy-start.1
  9.0 214.1 %all_to_all.5 = f32[8,288,1024]{2,1,0:T(8,128)S(1)} all-to-all(f32[8,288,1024]{2,1,0:T(8,128)S(1)} %stack.2), channel_id=1, replica_groups=mesh['depth'=32,'cols'=8] {'cols'}, dimensions={0} | all-to-all | bytes 18874368 | tf_op jit(solution)/shard_map/all_to_all | solution.py:9
  223.1 0.0 copy-done.1
  223.2 32.5 %fusion = f32[2304,1024]{1,0:T(8,128)} fusion(f32[2304,1024]{1,0:T(8,128)S(1)} %bitcast.3, f32[1024,1024]{1,0:T(8,128)S(1)} %copy-done.1), kind=kOutput, calls=%fused_computation | convolution fusion | flops 28991029248 | bytes 23068672 | tf_op jit(solution)/shard_map/dot_general | solution.py:11
  255.7 0.0 copy-start
  255.7 0.0 reduce-scatter.2.cloned.1.call-update
  255.7 186.4 %reduce-scatter.2.cloned.1.call-done = f32[72,1024]{1,0:T(8,128)} async-done(((f32[2304,1024]{1,0:T(8,128)}), f32[72,1024]{1,0:T(8,128)}) %reduce-scatter.2.cloned.1.call-update) | async-done | bytes 294928 | tf_op jit(solution)/shard_map/reduce_scatter | solution.py:14
  442.1 0.0 copy-done
  442.1 1.7 add.5
Async XLA Ops:
  6.5 435.6 %reduce-scatter.2.cloned.1.call-start = ((), (), s32[]{:S(2)}) async-start(), calls=%async_computation.2 | async-start | bytes 9732096 | tf_op jit(solution)/shard_map/reduce_scatter | solution.py:14
  9.0 214.2 %copy-start.1 = (f32[1024,1024]{1,0:T(8,128)S(1)}, f32[1024,1024]{1,0:T(8,128)}, u32[]{:S(2)}) copy-start(f32[1024,1024]{1,0:T(8,128)} %param.4) | copy-start | bytes 12582916
  255.7 186.4 %copy-start = (f32[72,1024]{1,0:T(8,128)S(1)}, f32[72,1024]{1,0:T(8,128)}, u32[]{:S(2)}) copy-start(f32[72,1024]{1,0:T(8,128)} %param.5) | copy-start | bytes 884740
Sparse Core Ops, SparseCore 0:
  255.8 186.2 reduce-scatter.1
